TPU v7x, 128 devices: a whole 4x4x4 slice. The times are simulated.
128 devices in a mesh: tok: 16 (over z, x), exp: 8 (over y, core).
Axes of the slice: x: 4, y: 4, z: 4, core: 2. Of those that a mesh axis runs over, the one named last changes fastest.
Arguments:
- tokens: bfloat16 [3072, 2048], P('tok'), may hold values from -6 to 6
- gain_attn: float32 [2048], replicated, may hold values from 0.5 to 1.5
- router_attn: bfloat16 [2048, 8], replicated, may hold values from -0.125 to 0.125
- kv_weight: bfloat16 [2048, 4096], P(None, 'exp')
- query_weight: bfloat16 [8, 2048, 2048], P('exp', None, 'tok')
- out_weight: bfloat16 [8, 2048, 2048], P('exp', 'tok'), may hold values from -0.125 to 0.125
- gain_mlp: float32 [2048], replicated, may hold values from 0.5 to 1.5
- router_mlp: bfloat16 [2048, 8], replicated, may hold values from -0.125 to 0.125
- gate_weight: bfloat16 [8, 2048, 5632], P('exp', None, 'tok'), may hold values from -0.125 to 0.125
- up_weight: bfloat16 [8, 2048, 5632], P('exp', None, 'tok'), may hold values from -0.125 to 0.125
- down_weight: bfloat16 [8, 5632, 2048], P('exp', 'tok'), may hold values from -0.078125 to 0.078125
- routes_attn: int32 [3072, 2], P('tok'), may hold values from 0 to 7, all different within a row; in each aligned block of 192 rows (0 to 191, 192 to 383, ...) at most 96 rows name the same one
- routes_mlp: int32 [3072, 2], P('tok'), may hold values from 0 to 7, all different within a row; in each aligned block of 192 rows (0 to 191, 192 to 383, ...) at most 96 rows name the same one
- lengths: int32 [3], replicated, may hold values from 256 to 1536, as said below
- page_table: int32 [3, 12, 2], replicated, may hold values from 0 to 15, as said below
Outputs:
- mixed: bfloat16 [3072, 2048], P('tok', 'exp')
- kv_pages: bfloat16 [32, 128, 4096], P('tok', None, 'exp')
Inputs may be any that keep to these rules, and one draw needn't show every extreme that they name: `routes_attn`: in each device's block of 192 tokens no expert is named by more than 96 tokens, a bound that some block reaches of them. `routes_mlp`: in each device's block of 192 tokens no expert is named by more than 96 tokens, a bound that some block reaches of them. The lengths sum to 3072; one prompt has exactly 1536 tokens. `page_table`: entry [s, i] holds (owner along tok, slot) of page i of prompt s, its tokens i * 128 to (i + 1) * 128 - 1; existing pages have distinct (owner, slot) pairs; the pages touched by one device's block of 192 tokens have distinct owners, so one block sends at most one page's tokens to an owner; entries past a prompt's last page are 0.
All inputs are finite; a program needn't handle non-finite values.
Results may differ from a plain program's by a relative error of at most 0.015.
The roundings to bfloat16 on the way count: a program that leaves them out, or rounds other values in their place, can miss the bound.
Values may be sent and summed in bfloat16 or wider, within the bound.
A program may use at most 128 MiB of HBM per device.

v0:
```python
import jax
import jax.numpy as jnp
from jax import lax
from jax.sharding import PartitionSpec as P

HD = 128
PAGE = 128
epsilon = 1e-06


def normalize(values, gain):
    return values * lax.rsqrt(jnp.mean(values * values, axis=-1, keepdims=True) + epsilon) * gain


def rotate(values, position):
    half_width = values.shape[-1] // 2
    exponent = jnp.arange(half_width, dtype=jnp.float32) * (2.0 / values.shape[-1])
    frequency = jnp.power(jnp.float32(10000.0), -exponent)
    angles = position.astype(jnp.float32)[:, None] * frequency[None, :]
    cosine = jnp.cos(angles)[:, None, :]
    sine_part = jnp.sin(angles)[:, None, :]
    leading = values[..., :half_width]
    trailing = values[..., half_width:]
    return jnp.concatenate(
        [leading * cosine - trailing * sine_part, trailing * cosine + leading * sine_part], axis=-1
    )


def locate(lengths, number):
    segment_ends = jnp.cumsum(lengths)
    segment_starts = segment_ends - lengths
    segment = jnp.sum((number[:, None] >= segment_ends[None, :]).astype(jnp.int32), axis=1)
    matched = segment[:, None] == jnp.arange(lengths.shape[0], dtype=jnp.int32)[None, :]
    start_of = jnp.sum(jnp.where(matched, segment_starts[None, :], 0), axis=1)
    return (segment, (number - start_of).astype(jnp.int32), start_of)


def pair_gates(logits, routes):
    leading = jnp.take_along_axis(logits, routes[:, 0:1], axis=1)[:, 0]
    trailing = jnp.take_along_axis(logits, routes[:, 1:2], axis=1)[:, 0]
    return (jax.nn.sigmoid(leading - trailing), jax.nn.sigmoid(trailing - leading))


def compact(routes, leading, trailing, expert, capacity):
    count_rows = routes.shape[0]
    chosen = (routes[:, 0] == expert) | (routes[:, 1] == expert)
    weight = jnp.where(routes[:, 0] == expert, leading, 0.0) + jnp.where(
        routes[:, 1] == expert, trailing, 0.0
    )
    ranking = jnp.cumsum(chosen.astype(jnp.int32)) - 1
    slot_rank = jnp.arange(capacity, dtype=jnp.int32)
    matches = chosen[None, :] & (ranking[None, :] == slot_rank[:, None])
    picked = jnp.sum(
        jnp.where(matches, jnp.arange(count_rows, dtype=jnp.int32)[None, :], 0), axis=1
    )
    filled = slot_rank < jnp.sum(chosen.astype(jnp.int32))
    return (picked, jnp.where(filled, jnp.take(weight, picked), 0.0))


def spread_rows(picked, contribution, count_rows):
    placing = (jnp.arange(count_rows, dtype=jnp.int32)[:, None] == picked[None, :]).astype(
        jnp.float32
    )
    return jnp.dot(placing, contribution, precision=lax.Precision.HIGHEST)


def attend(queries, query_number, query_segment, key_heads, value_heads, key_segment):
    query_total = queries.shape[0]
    key_total = key_heads.shape[0]
    query_groups = max(1, query_total // 512)
    query_rows = query_total // query_groups
    key_groups = max(1, key_total // 512)
    key_rows = key_total // key_groups
    score_scale = queries.shape[-1] ** (-0.5)
    heads_here = queries.shape[1]
    key_number = jnp.arange(key_total, dtype=jnp.int32)
    results = []
    for query_group in range(query_groups):
        row_begin = query_group * query_rows
        query_part = queries[row_begin : row_begin + query_rows]
        number_part = query_number[row_begin : row_begin + query_rows]
        segment_part = query_segment[row_begin : row_begin + query_rows]

        def visit(counter, running):
            highest, denominator, summed = running
            first_key = counter * key_rows
            key_part = lax.dynamic_slice_in_dim(key_heads, first_key, key_rows, 0)
            value_part = lax.dynamic_slice_in_dim(value_heads, first_key, key_rows, 0)
            segment_keys = lax.dynamic_slice_in_dim(key_segment, first_key, key_rows, 0)
            number_keys = lax.dynamic_slice_in_dim(key_number, first_key, key_rows, 0)
            allowed = (segment_keys[None, :] == segment_part[:, None]) & (
                number_keys[None, :] <= number_part[:, None]
            )
            scores = (
                jnp.einsum("qhd,khd->hqk", query_part, key_part, preferred_element_type=jnp.float32)
                * score_scale
            )
            scores = jnp.where(allowed[None], scores, -1e30)
            newest = jnp.maximum(highest, jnp.max(scores, axis=2))
            weights = jnp.where(allowed[None], jnp.exp(scores - newest[:, :, None]), 0.0)
            shrink = jnp.exp(highest - newest)
            denominator = denominator * shrink + jnp.sum(weights, axis=2)
            summed = summed * shrink[:, :, None] + jnp.einsum(
                "hqk,khd->hqd",
                weights.astype(jnp.bfloat16),
                value_part,
                preferred_element_type=jnp.float32,
            )
            return (newest, denominator, summed)

        start_state = (
            jnp.full((heads_here, query_rows), -1e30, jnp.float32),
            jnp.zeros((heads_here, query_rows), jnp.float32),
            jnp.zeros((heads_here, query_rows, queries.shape[-1]), jnp.float32),
        )
        highest, denominator, summed = lax.fori_loop(0, key_groups, visit, start_state)
        results.append(jnp.swapaxes((summed / denominator[:, :, None]).astype(jnp.bfloat16), 0, 1))
    return jnp.concatenate(results, axis=0)


def shards(
    tokens,
    gain_attn,
    router_attn,
    kv_weight,
    query_weight,
    out_weight,
    gain_mlp,
    router_mlp,
    gate_weight,
    up_weight,
    down_weight,
    routes_attn,
    routes_mlp,
    lengths,
    page_table,
):
    tok_count = lax.axis_size("tok")
    exp_count = lax.axis_size("exp")
    tok_rank = lax.axis_index("tok")
    exp_rank = lax.axis_index("exp")
    rows_here, model_width = tokens.shape
    head_size = HD
    heads_kv = kv_weight.shape[1] // (2 * head_size)
    heads_here = query_weight.shape[2] // head_size
    capacity = rows_here // 2
    total_tokens = rows_here * tok_count
    page_rows = PAGE
    pages_each = page_table.shape[1]
    slot_count = (total_tokens // page_rows + lengths.shape[0]) // tok_count + 1
    widened = tokens.astype(jnp.float32)
    normed = normalize(widened, gain_attn).astype(jnp.bfloat16)
    own_number = tok_rank * rows_here + jnp.arange(rows_here, dtype=jnp.int32)
    own_segment, own_offset, own_start = locate(lengths, own_number)
    projected_kv = jnp.dot(normed, kv_weight, preferred_element_type=jnp.float32).reshape(
        rows_here, heads_kv, 2, head_size
    )
    rotated = rotate(projected_kv[:, :, 0], own_offset)
    paired = (
        jnp.stack([rotated, projected_kv[:, :, 1]], axis=2)
        .astype(jnp.bfloat16)
        .reshape(rows_here, heads_kv * 2 * head_size)
    )
    entries = jnp.take(
        page_table.reshape(-1, 2), own_segment * pages_each + own_offset // page_rows, axis=0
    )
    owner_of = entries[:, 0]
    slot_of = entries[:, 1]
    placed = owner_of * page_rows + own_offset % page_rows
    selector = (
        jnp.arange(tok_count * page_rows, dtype=jnp.int32)[:, None] == placed[None, :]
    ).astype(jnp.bfloat16)
    outgoing = (
        jnp.dot(selector, paired, preferred_element_type=jnp.float32)
        .astype(jnp.bfloat16)
        .reshape(tok_count, page_rows, -1)
    )
    owner_hits = owner_of[None, :] == jnp.arange(tok_count, dtype=jnp.int32)[:, None]
    slot_sent = jnp.max(jnp.where(owner_hits, slot_of[None, :], 0), axis=1).reshape(tok_count, 1)
    arrived, arrived_slot = (
        lax.all_to_all(outgoing, "tok", split_axis=0, concat_axis=0, tiled=True),
        lax.all_to_all(slot_sent, "tok", split_axis=0, concat_axis=0, tiled=True),
    )
    filing = (
        jnp.arange(slot_count, dtype=jnp.int32)[:, None] == arrived_slot[:, 0][None, :]
    ).astype(jnp.bfloat16)
    kv_pages = (
        jnp.dot(filing, arrived.reshape(tok_count, -1), preferred_element_type=jnp.float32)
        .astype(jnp.bfloat16)
        .reshape(slot_count, page_rows, -1)
    )
    all_heads = lax.all_gather(paired, "exp", axis=1, tiled=True)
    regrouped = lax.all_to_all(
        all_heads.reshape(rows_here, tok_count, heads_here * 2 * head_size),
        "tok",
        split_axis=1,
        concat_axis=0,
        tiled=True,
    )
    regrouped = regrouped.reshape(total_tokens, heads_here, 2, head_size)
    key_heads = regrouped[:, :, 0]
    value_heads = regrouped[:, :, 1]
    key_segment, key_offset, key_start = locate(lengths, jnp.arange(total_tokens, dtype=jnp.int32))
    attn_logits = jnp.dot(normed, router_attn, preferred_element_type=jnp.float32)
    leading, trailing = pair_gates(attn_logits, routes_attn)
    picked, attn_gate = compact(routes_attn, leading, trailing, exp_rank, capacity)
    chosen_rows = jnp.take(normed, picked, axis=0)
    chosen_number = tok_rank * rows_here + picked
    query_full = jnp.dot(
        chosen_rows,
        lax.all_gather(query_weight[0], "tok", axis=1, tiled=True),
        preferred_element_type=jnp.float32,
    )
    chosen_segment, chosen_offset, chosen_start = locate(lengths, chosen_number)
    query_local = rotate(query_full.reshape(capacity, -1, head_size), chosen_offset).astype(
        jnp.bfloat16
    )
    number_copies = jnp.broadcast_to(chosen_number[:, None], (capacity, tok_count))
    query_heads, query_number = (
        lax.all_to_all(query_local, "tok", split_axis=1, concat_axis=0, tiled=True),
        lax.all_to_all(number_copies, "tok", split_axis=1, concat_axis=0, tiled=True),
    )
    query_number = query_number.reshape(-1)
    query_segment, query_offset, query_start = locate(lengths, query_number)
    attended = attend(query_heads, query_number, query_segment, key_heads, value_heads, key_segment)
    returned = lax.all_to_all(
        attended.reshape(tok_count, capacity, heads_here * head_size),
        "tok",
        split_axis=0,
        concat_axis=2,
        tiled=True,
    )
    returned = returned.reshape(capacity, -1)
    mixed_attn = jnp.dot(
        returned,
        lax.all_gather(out_weight[0], "tok", axis=0, tiled=True),
        preferred_element_type=jnp.float32,
    )
    attn_rows = spread_rows(picked, mixed_attn * attn_gate[:, None], rows_here)
    share_width = model_width // exp_count
    first_column = exp_rank * share_width
    attn_total = lax.psum(attn_rows.astype(jnp.bfloat16), "exp").astype(jnp.float32)
    residual = widened + attn_total
    normed_mlp = normalize(residual, gain_mlp).astype(jnp.bfloat16)
    residual_share = lax.dynamic_slice_in_dim(residual, first_column, share_width, 1)
    mlp_logits = jnp.dot(normed_mlp, router_mlp, preferred_element_type=jnp.float32)
    leading_mlp, trailing_mlp = pair_gates(mlp_logits, routes_mlp)
    picked_mlp, mlp_gate = compact(routes_mlp, leading_mlp, trailing_mlp, exp_rank, capacity)
    expert_input = jnp.take(normed_mlp, picked_mlp, axis=0)
    portion = lax.all_gather(expert_input, "tok", axis=0, tiled=True)
    gate_part = jnp.dot(portion, gate_weight[0], preferred_element_type=jnp.float32)
    upward = jnp.dot(portion, up_weight[0], preferred_element_type=jnp.float32)
    hidden = (jax.nn.silu(gate_part) * upward).astype(jnp.bfloat16)
    expert_out = lax.psum_scatter(
        jnp.dot(hidden, down_weight[0], preferred_element_type=jnp.float32).astype(jnp.bfloat16),
        "tok",
        scatter_dimension=0,
        tiled=True,
    ).astype(jnp.float32)
    expert_local = spread_rows(picked_mlp, expert_out * mlp_gate[:, None], rows_here)
    expert_share = lax.psum_scatter(
        expert_local.astype(jnp.bfloat16), "exp", scatter_dimension=1, tiled=True
    ).astype(jnp.float32)
    mixed = (residual_share + expert_share).astype(jnp.bfloat16)
    return (mixed, kv_pages)


def solution(mesh):
    return jax.shard_map(
        shards,
        mesh=mesh,
        in_specs=(
            P("tok", None),
            P(),
            P(),
            P(None, "exp"),
            P("exp", None, "tok"),
            P("exp", "tok", None),
            P(),
            P(),
            P("exp", None, "tok"),
            P("exp", None, "tok"),
            P("exp", "tok", None),
            P("tok", None),
            P("tok", None),
            P(),
            P(),
        ),
        out_specs=(P("tok", "exp"), P("tok", None, "exp")),
        check_vma=False,
    )
```

profile of v0, /device:TPU:0, one launch (start us, length us, event | category | flops | bytes accessed | tf_op | source)
XLA Modules:
  0.0 524.7 jit_solution(327691876324778887)
XLA Ops:
  18.7 8.0 %all-to-all-start = ((s32[96,16,1]{0,2,1:T(1,128)}), s32[96,16,1]{0,2,1:T(1,128)S(1)}, u32[]{:S(2)}, u32[]{:S(2)}) async-start(s32[96,16,1]{0,2,1:T(1,128)} %broadcast_in_dim.247), calls=%async_computation | async-start | bytes 16384 | tf_op jit(solution)/shard_map/all_to_all | solution.py:221
  32.3 11.2 %all-gather.7.cloned.1.call-done = bf16[192,4096]{1,0:T(8,128)(2,1)} async-done(((bf16[192,512]{1,0:T(8,128)(2,1)}), bf16[192,4096]{1,0:T(8,128)(2,1)}) %all-gather.7.cloned.1.call-update) | async-done | bytes 1572880 | tf_op jit(solution)/shard_map/all_gather | solution.py:192
  43.5 2.7 copy.93
  46.2 6.9 %all-to-all-start.1 = ((bf16[192,16,256]{2,0,1:T(8,128)(2,1)}), bf16[192,16,256]{2,0,1:T(8,128)(2,1)S(1)}, u32[]{:S(2)}, u32[]{:S(2)}) async-start(bf16[192,16,256]{2,0,1:T(8,128)(2,1)} %bitcast.202), calls=%async_computation.1 | async-start | bytes 3145728 | tf_op jit(solution)/shard_map/all_to_all | solution.py:193
  59.1 25.7 %all-to-all-done.1 = bf16[192,16,256]{2,0,1:T(8,128)(2,1)S(1)} async-done(((bf16[192,16,256]{2,0,1:T(8,128)(2,1)}), bf16[192,16,256]{2,0,1:T(8,128)(2,1)S(1)}, u32[]{:S(2)}, u32[]{:S(2)}) %all-to-all-start.1) | async-done | bytes 1572896 | tf_op jit(solution)/shard_map/all_to_all | solution.py:193
  85.9 2.4 reshape.595
  88.3 3.5 fusion.139
  91.8 43.1 %all-gather.11.cloned.1.call-done = bf16[1,2048,2048]{2,1,0:T(8,128)(2,1)} async-done(((bf16[1,2048,128]{2,1,0:T(8,128)(2,1)}), bf16[1,2048,2048]{2,1,0:T(8,128)(2,1)}) %all-gather.11.cloned.1.call-update) | async-done | bytes 8388624 | tf_op jit(solution)/shard_map/all_gather | solution.py:211
  134.9 4.9 fusion.84
  141.7 5.0 all-to-all-start.2
  146.7 2.7 copy_bitcast_fusion.1
  149.4 10.8 %all-to-all-done.2 = bf16[96,16,128]{2,0,1:T(8,128)(2,1)S(1)} async-done(((bf16[96,16,128]{2,0,1:T(8,128)(2,1)}), bf16[96,16,128]{2,0,1:T(8,128)(2,1)S(1)}, u32[]{:S(2)}, u32[]{:S(2)}) %all-to-all-start.2) | async-done | bytes 393248 | tf_op jit(solution)/shard_map/all_to_all | solution.py:220
  161.0 19.0 %while.54 = (s32[]{:T(128)}, f32[1,512]{1,0:T(1,128)S(1)}, f32[1,512]{1,0:T(1,128)S(1)}, f32[1,512,128]{2,1,0:T(8,128)}, s32[3072]{0:T(1024)S(1)}, /*index=5*/s3...) while((s32[]{:T(128)}, f32[1,512]{1,0:T(1,128)S(1)}, ...), condition=%wide.region_14.16_spmd.clone, body=%wide.region_11.15_spmd.clone.sunk | while | flops 139135488 | bytes 6226191 | solution.py:116
  181.1 14.5 %while.55 = (s32[]{:T(128)}, f32[1,512]{1,0:T(1,128)S(1)}, f32[1,512]{1,0:T(1,128)S(1)}, f32[1,512,128]{2,1,0:T(8,128)S(1)}, s32[3072]{0:T(1024)S(1)}, /*index=5...) while((s32[]{:T(128)}, f32[1,512]{1,0:T(1,128)S(1)}, ...), condition=%wide.region_18.20_spmd.clone, body=%wide.region_15.19_spmd.clone.sunk | while | flops 139135488 | bytes 4128983 | solution.py:116
  195.8 14.5 %while.56 = (s32[]{:T(128)}, f32[1,512]{1,0:T(1,128)S(1)}, f32[1,512]{1,0:T(1,128)S(1)}, f32[1,512,128]{2,1,0:T(8,128)S(1)}, s32[3072]{0:T(1024)S(1)}, /*index=5...) while((s32[]{:T(128)}, f32[1,512]{1,0:T(1,128)S(1)}, ...), condition=%wide.region_22.24_spmd.clone, body=%wide.region_19.23_spmd.clone.sunk | while | flops 139135488 | bytes 4128983 | solution.py:116
  211.3 3.6 all-to-all-start.3
  215.1 9.2 %all-to-all-done.3 = bf16[16,96,128]{2,1,0:T(8,128)(2,1)S(1)} async-done(((bf16[16,96,128]{2,1,0:T(8,128)(2,1)}), bf16[16,96,128]{2,1,0:T(8,128)(2,1)S(1)}, u32[]{:S(2)}, u32[]{:S(2)}) %all-to-all-start.3) | async-done | bytes 393248 | tf_op jit(solution)/shard_map/all_to_all | solution.py:226
  224.5 4.8 fusion.74
  229.4 1.7 convolution_convert_fusion.4
  231.8 58.7 %all-reduce.4.cloned.1.call-done = bf16[192,2048]{1,0:T(8,128)(2,1)} async-done(((bf16[192,2048]{1,0:T(8,128)(2,1)}), bf16[192,2048]{1,0:T(8,128)(2,1)}) %all-reduce.4.cloned.1.call-update) | async-done | bytes 786448 | tf_op jit(solution)/shard_map/psum | solution.py:242
  290.5 2.6 convert_add_fusion
  301.3 60.5 %all-gather.9.cloned.1.call-done = bf16[1536,2048]{1,0:T(8,128)(2,1)} async-done(((bf16[96,2048]{1,0:T(8,128)(2,1)}), bf16[1536,2048]{1,0:T(8,128)(2,1)}) %all-gather.9.cloned.1.call-update) | async-done | bytes 6291472 | tf_op jit(solution)/shard_map/all_gather | solution.py:250
  361.8 6.6 %fusion.82 = f32[1536,352]{0,1:T(8,128)} fusion(bf16[1536,2048]{1,0:T(8,128)(2,1)} %all-gather.9.cloned.1.call-done, bf16[1,2048,352]{1,2,0:T(8,128)(2,1)S(1)} %copy-done.33), kind=kOutput, calls=%fused_computation.123 | convolution fusion | flops 2214592512 | bytes 9895936 | tf_op jit(solution)/shard_map/dot_general | solution.py:251
  368.4 11.9 %convolution_convert_fusion.1 = bf16[1536,2048]{1,0:T(8,128)(2,1)} fusion(bf16[1,352,2048]{2,1,0:T(8,128)(2,1)S(1)} %copy-done.34, bf16[1536,2048]{1,0:T(8,128)(2,1)} %all-gather.9.cloned.1.call-done, f32[1536,352]{0,1:T(8,128)} %fusion.82, bf16[1,2048,352]{1,2,0:T(8,128)(2,1)} %param.36), kind=kOutput, calls=%fused_computation.104 | convolution fusion | flops 4435574784 | bytes 17629184 | tf_op jit(solution)/shard_map/dot_general | solution.py:255
  381.7 5.3 %all-to-all-start.4 = ((s32[16,1,1]{2,1,0:T(1,128)}), s32[16,1,1]{2,1,0:T(1,128)S(1)}, u32[]{:S(2)}, u32[]{:S(2)}) async-start(s32[16,1,1]{2,1,0:T(1,128)} %copy.66), calls=%async_computation.6 | async-start | bytes 16384 | tf_op jit(solution)/shard_map/all_to_all | solution.py:182
  387.0 2.1 convolution_convert_fusion.2
  389.1 5.4 %all-to-all-done.4 = s32[16,1,1]{2,1,0:T(1,128)S(1)} async-done(((s32[16,1,1]{2,1,0:T(1,128)}), s32[16,1,1]{2,1,0:T(1,128)S(1)}, u32[]{:S(2)}, u32[]{:S(2)}) %all-to-all-start.4) | async-done | bytes 96 | tf_op jit(solution)/shard_map/all_to_all | solution.py:182
  394.5 3.7 all-to-all-start.5
  398.3 83.9 %reduce-scatter.3.cloned.1.call-done = bf16[96,2048]{1,0:T(8,128)(2,1)} async-done(((bf16[1536,2048]{1,0:T(8,128)(2,1)}), bf16[96,2048]{1,0:T(8,128)(2,1)}) %reduce-scatter.3.cloned.1.call-update) | async-done | bytes 393232 | tf_op jit(solution)/shard_map/reduce_scatter | solution.py:254
  482.2 2.8 convolution_convert_fusion.3
  487.7 28.4 %reduce-scatter.5.cloned.1.call-done = bf16[192,256]{1,0:T(8,128)(2,1)} async-done(((bf16[192,2048]{1,0:T(8,128)(2,1)}), bf16[192,256]{1,0:T(8,128)(2,1)}) %reduce-scatter.5.cloned.1.call-update) | async-done | bytes 98320 | tf_op jit(solution)/shard_map/reduce_scatter | solution.py:261
  516.2 1.6 add_convert_fusion.1
  (372 shorter events, 89.0 us)
Async XLA Ops:
  7.2 36.3 %all-gather.7.cloned.1.call-start = ((), (), s32[]{:S(2)}) async-start(), calls=%async_computation.8 | async-start | bytes 1769472 | tf_op jit(solution)/shard_map/all_gather | solution.py:192
  15.3 12.3 %copy-start.17 = (s32[192,2]{0,1:T(2,128)S(1)}, s32[192,2]{0,1:T(2,128)}, u32[]{:S(2)}) copy-start(s32[192,2]{0,1:T(2,128)} %param.39) | copy-start | bytes 4612
  15.4 12.3 %copy-start.14 = (bf16[2048,8]{0,1:T(8,128)(2,1)S(1)}, bf16[2048,8]{0,1:T(8,128)(2,1)}, u32[]{:S(2)}) copy-start(bf16[2048,8]{0,1:T(8,128)(2,1)} %param.29) | copy-start | bytes 98308
  16.5 118.3 %all-gather.11.cloned.1.call-start = ((), (), s32[]{:S(2)}) async-start(), calls=%async_computation.13 | async-start | bytes 8912896 | tf_op jit(solution)/shard_map/all_gather | solution.py:211
  18.1 38.1 %copy-start.22 = (s32[96]{0:T(128)}, s32[96]{0:T(128)S(1)}, u32[]{:S(2)}) copy-start(s32[96]{0:T(128)S(1)} %select_reduce_fusion.1) | copy-start | bytes 1156
  18.7 27.5 %all-to-all-start = ((s32[96,16,1]{0,2,1:T(1,128)}), s32[96,16,1]{0,2,1:T(1,128)S(1)}, u32[]{:S(2)}, u32[]{:S(2)}) async-start(s32[96,16,1]{0,2,1:T(1,128)} %broadcast_in_dim.247), calls=%async_computation | async-start | bytes 16384 | tf_op jit(solution)/shard_map/all_to_all | solution.py:221
  26.7 197.8 %all-gather.13.cloned.1.call-start = ((), (), s32[]{:S(2)}) async-start(), calls=%async_computation.14 | async-start | bytes 8912896 | tf_op jit(solution)/shard_map/all_gather | solution.py:236
  46.2 38.5 %all-to-all-start.1 = ((bf16[192,16,256]{2,0,1:T(8,128)(2,1)}), bf16[192,16,256]{2,0,1:T(8,128)(2,1)S(1)}, u32[]{:S(2)}, u32[]{:S(2)}) async-start(bf16[192,16,256]{2,0,1:T(8,128)(2,1)} %bitcast.202), calls=%async_computation.1 | async-start | bytes 3145728 | tf_op jit(solution)/shard_map/all_to_all | solution.py:193
  140.7 6.0 %copy-start.4 = (bf16[3072,1,1,128]{3,2,0,1:T(2,128)(2,1)S(1)}, bf16[3072,1,1,128]{3,2,0,1:T(2,128)(2,1)}, u32[]{:S(2)}) copy-start(bf16[3072,1,1,128]{3,2,0,1:T(2,128)(2,1)} %get-tuple-element.762) | copy-start | bytes 2359300
  141.7 18.5 %all-to-all-start.2 = ((bf16[96,16,128]{2,0,1:T(8,128)(2,1)}), bf16[96,16,128]{2,0,1:T(8,128)(2,1)S(1)}, u32[]{:S(2)}, u32[]{:S(2)}) async-start(bf16[96,16,128]{2,0,1:T(8,128)(2,1)} %pad_maximum_fusion), calls=%async_computation.2 | async-start | bytes 786432 | tf_op jit(solution)/shard_map/all_to_all | solution.py:220
  146.7 14.2 %copy-start.10 = (s32[512]{0:T(512)S(1)}, s32[512]{0:T(512)}, u32[]{:S(2)}) copy-start(s32[512]{0:T(512)} %get-tuple-element.1122) | copy-start | bytes 6148
  146.7 14.2 %copy-start.13 = (f32[1,512]{1,0:T(1,128)S(1)}, f32[1,512]{1,0:T(1,128)}, u32[]{:S(2)}) copy-start(f32[1,512]{1,0:T(1,128)} %custom-call.9) | copy-start | bytes 6148
  161.0 20.1 %copy-start.9 = (bf16[512,1,128]{2,0,1:T(8,128)(2,1)S(1)}, bf16[512,1,128]{2,0,1:T(8,128)(2,1)}, u32[]{:S(2)}) copy-start(bf16[512,1,128]{2,0,1:T(8,128)(2,1)} %get-tuple-element.1081) | copy-start | bytes 393220
  161.0 20.1 %copy-start.12 = (f32[1,512]{1,0:T(1,128)S(1)}, f32[1,512]{1,0:T(1,128)}, u32[]{:S(2)}) copy-start(f32[1,512]{1,0:T(1,128)} %custom-call.12) | copy-start | bytes 6148
  181.1 14.7 %copy-start.11 = (f32[1,512]{1,0:T(1,128)S(1)}, f32[1,512]{1,0:T(1,128)}, u32[]{:S(2)}) copy-start(f32[1,512]{1,0:T(1,128)} %custom-call.15) | copy-start | bytes 6148
  210.4 4.6 copy-start.32
  210.4 14.1 %copy-start.30 = (f32[96]{0:T(128)S(1)}, f32[96]{0:T(128)}, u32[]{:S(2)}) copy-start(f32[96]{0:T(128)} %get-tuple-element.750) | copy-start | bytes 1156
  211.3 12.9 %all-to-all-start.3 = ((bf16[16,96,128]{2,1,0:T(8,128)(2,1)}), bf16[16,96,128]{2,1,0:T(8,128)(2,1)S(1)}, u32[]{:S(2)}, u32[]{:S(2)}) async-start(bf16[16,96,128]{2,1,0:T(8,128)(2,1)} %bitcast.21), calls=%async_computation.3 | async-start | bytes 786432 | tf_op jit(solution)/shard_map/all_to_all | solution.py:226
  214.9 75.6 %all-reduce.4.cloned.1.call-start = ((), (), s32[]{:S(2)}) async-start(), calls=%async_computation.9 | async-start | bytes 1572864 | tf_op jit(solution)/shard_map/psum | solution.py:242
  224.5 4.9 copy-start.23
  229.3 61.2 %copy-start.2 = (bf16[192,2048]{1,0:T(8,128)(2,1)S(1)}, bf16[192,2048]{1,0:T(8,128)(2,1)}, u32[]{:S(2)}) copy-start(bf16[192,2048]{1,0:T(8,128)(2,1)} %param.27) | copy-start | bytes 2359300
  231.1 130.7 %all-gather.9.cloned.1.call-start = ((), (), s32[]{:S(2)}) async-start(), calls=%async_computation.10 | async-start | bytes 6684672 | tf_op jit(solution)/shard_map/all_gather | solution.py:250
  231.8 61.4 %copy-start.21 = (f32[2048]{0:T(1024)S(1)}, f32[2048]{0:T(1024)}, u32[]{:S(2)}) copy-start(f32[2048]{0:T(1024)} %param.33) | copy-start | bytes 24580
  298.1 63.7 %copy-start.33 = (bf16[1,2048,352]{1,2,0:T(8,128)(2,1)S(1)}, bf16[1,2048,352]{1,2,0:T(8,128)(2,1)}, u32[]{:S(2)}) copy-start(bf16[1,2048,352]{1,2,0:T(8,128)(2,1)} %param.35) | copy-start | bytes 4325380
  301.0 67.4 %copy-start.34 = (bf16[1,352,2048]{2,1,0:T(8,128)(2,1)S(1)}, bf16[1,352,2048]{2,1,0:T(8,128)(2,1)}, u32[]{:S(2)}) copy-start(bf16[1,352,2048]{2,1,0:T(8,128)(2,1)} %param.37) | copy-start | bytes 4325380
  301.0 181.2 %reduce-scatter.3.cloned.1.call-start = ((), (), s32[]{:S(2)}) async-start(), calls=%async_computation.11 | async-start | bytes 6684672 | tf_op jit(solution)/shard_map/reduce_scatter | solution.py:254
  380.2 6.8 %copy-start.6 = (bf16[192,512]{1,0:T(8,128)(2,1)S(1)}, bf16[192,512]{1,0:T(8,128)(2,1)}, u32[]{:S(2)}) copy-start(bf16[192,512]{1,0:T(8,128)(2,1)} %convert_element_type.123) | copy-start | bytes 589828
  380.3 6.8 %copy-start.27 = (s32[192]{0:T(256)S(1)}, s32[192]{0:T(256)}, u32[]{:S(2)}) copy-start(s32[192]{0:T(256)} %get-tuple-element.783) | copy-start | bytes 2308
  381.7 12.8 %all-to-all-start.4 = ((s32[16,1,1]{2,1,0:T(1,128)}), s32[16,1,1]{2,1,0:T(1,128)S(1)}, u32[]{:S(2)}, u32[]{:S(2)}) async-start(s32[16,1,1]{2,1,0:T(1,128)} %copy.66), calls=%async_computation.6 | async-start | bytes 16384 | tf_op jit(solution)/shard_map/all_to_all | solution.py:182
  394.5 90.9 %all-to-all-start.5 = ((bf16[16,128,512]{2,1,0:T(8,128)(2,1)}), bf16[16,128,512]{2,1,0:T(8,128)(2,1)S(1)}, u32[]{:S(2)}, u32[]{:S(2)}) async-start(bf16[16,128,512]{2,1,0:T(8,128)(2,1)} %bitcast.52), calls=%async_computation.7 | async-start | bytes 4194304 | tf_op jit(solution)/shard_map/all_to_all | solution.py:181
  398.2 117.9 %reduce-scatter.5.cloned.1.call-start = ((), (), s32[]{:S(2)}) async-start(), calls=%async_computation.12 | async-start | bytes 884736 | tf_op jit(solution)/shard_map/reduce_scatter | solution.py:261
  486.5 31.3 %copy-start.1 = (bf16[2048,512]{1,0:T(8,128)(2,1)S(1)}, bf16[2048,512]{1,0:T(8,128)(2,1)}, u32[]{:S(2)}) copy-start(bf16[2048,512]{1,0:T(8,128)(2,1)} %param.30) | copy-start | bytes 6291460
  (27 other events, 43.6 us)
Sparse Core Ops, SparseCore 0:
  16.6 26.8 all-gather.6
  45.6 89.1 all-gather.10
  137.0 72.2 all-gather.12
  231.2 59.2 all-reduce.3
  301.1 60.6 all-gather.8
  380.4 101.7 reduce-scatter.2
  485.1 31.0 reduce-scatter.4
where the time goes:
time: 526 us; the launch traced here: 525 us
  waiting for transfers between devices  338 us (64%)
  matrix products  70.3 us (13%)
  local copies, waits for them, and re-layouts  40.2 us (8%)
  starting transfers between devices  32.9 us (6%)
  other arithmetic  26.8 us (5%)
  between operations  15 us (3%)
    reduce_scatter x1, waiting for transfers between devices, shards(): lax.psum_scatter(jnp.dot(hidden, down_weight[0], preferred_element_type=j...  83.9 us
    all_gather x1, waiting for transfers between devices, shards(): portion = lax.all_gather(expert_input, 'tok', axis=0, tiled=True)  60.5 us
    psum x1, waiting for transfers between devices, shards(): lax.psum(attn_rows.astype(jnp.bfloat16), 'exp').astype(jnp.float32)  58.7 us
    all_gather x1, waiting for transfers between devices, shards(): lax.all_gather(query_weight[0], 'tok', axis=1, tiled=True)  43.1 us
    reduce_scatter x1, waiting for transfers between devices, shards(): lax.psum_scatter(expert_local.astype(jnp.bfloat16), 'exp', scatter_dimens...  28.4 us
    all_to_all x1, waiting for transfers between devices, shards(): lax.all_to_all(all_heads.reshape(rows_here, tok_count, heads_here * 2 * h...  25.7 us
    dot_general x18, matrix products, visit(): jnp.einsum('qhd,khd->hqk', query_part, key_part, preferred_element_type=j...  23.6 us
    dot_general x1, matrix products, shards(): jnp.dot(hidden, down_weight[0], preferred_element_type=jnp.float32)  11.9 us
  transfers between devices with their start and end apart: 13, of which 10 were waited for; matrix products, arithmetic and copies ran while one was open for 16% of the time, Pallas kernels for 0%

commit v1 on v0

--- a/solution.py
+++ b/solution.py
@@ -6,6 +6,28 @@
 HD = 128
 PAGE = 128
 epsilon = 1e-06
+
+
+def laid_out(blocks, dim):
+    blocks = jnp.moveaxis(blocks, 0, dim)
+    shape = blocks.shape
+    return blocks.reshape(*shape[:dim], shape[dim] * shape[dim + 1], *shape[dim + 2 :])
+
+
+def ring_gather(value, axis, dim):
+    size = lax.axis_size(axis)
+    pairs = [(i, (i + 1) % size) for i in range(size)]
+    back = [(b, a) for a, b in pairs]
+    lower, upper = ([], [])
+    for step in range(size - 1):
+        if step % 2 == 0:
+            lower.append(lax.ppermute(lower[-1] if lower else value, axis, pairs))
+        else:
+            upper.append(lax.ppermute(upper[-1] if upper else value, axis, back))
+    blocks = jnp.stack([*lower[::-1], value, *upper])
+    shift = lax.axis_index(axis) - len(lower)
+    blocks = blocks[(jnp.arange(size) - shift) % size]
+    return laid_out(blocks, dim)
 
 
 def normalize(values, gain):
@@ -189,7 +211,7 @@
         .astype(jnp.bfloat16)
         .reshape(slot_count, page_rows, -1)
     )
-    all_heads = lax.all_gather(paired, "exp", axis=1, tiled=True)
+    all_heads = ring_gather(paired, "exp", 1)
     regrouped = lax.all_to_all(
         all_heads.reshape(rows_here, tok_count, heads_here * 2 * head_size),
         "tok",

time: 526 us -> 499 us (0.949)
  waiting for transfers between devices: 338 us -> 301 us
  starting transfers between devices: 32.9 us -> 41.8 us
    all_gather x1, waiting for transfers between devices: 43.1 us -> 4.45 us  [shards(): lax.all_gather(query_weight[0], 'tok', axis=1, tiled=True)]
    ppermute x0 -> x7, waiting for transfers between devices: none -> 12.5 us  [the longest x4 12.4 us: ring_gather(): lower.append(lax.ppermute(lower[-1] if lower else value, axis, pairs))]
    all_gather x1 -> x0, waiting for transfers between devices: 11.2 us -> none  [shards(): all_heads = lax.all_gather(paired, 'exp', axis=1, tiled=True)]
    ppermute x0 -> x7, starting transfers between devices: none -> 9.06 us  [the longest x3 9.02 us: ring_gather(): upper.append(lax.ppermute(upper[-1] if upper else value, axis, back))]
  transfers between devices with their start and end apart: 13 -> 19, of which waited for: 10 -> 12; matrix products, arithmetic and copies ran while one was open for 16% -> 19% of each run, Pallas kernels for 0% -> 0%
where the time goes in v1:
time: 499 us; the launch traced here: 498 us
  waiting for transfers between devices  301 us (60%)
  matrix products  70.8 us (14%)
  local copies, waits for them, and re-layouts  43.6 us (9%)
  starting transfers between devices  41.8 us (8%)
  other arithmetic  25.2 us (5%)
  between operations  14.8 us (3%)
    reduce_scatter x1, waiting for transfers between devices, shards(): lax.psum_scatter(jnp.dot(hidden, down_weight[0], preferred_element_type=j...  83.7 us
    psum x1, waiting for transfers between devices, shards(): lax.psum(attn_rows.astype(jnp.bfloat16), 'exp').astype(jnp.float32)  61.8 us
    all_gather x1, waiting for transfers between devices, shards(): portion = lax.all_gather(expert_input, 'tok', axis=0, tiled=True)  60.7 us
    reduce_scatter x1, waiting for transfers between devices, shards(): lax.psum_scatter(expert_local.astype(jnp.bfloat16), 'exp', scatter_dimens...  28.4 us
    dot_general x18, matrix products, visit(): jnp.einsum('qhd,khd->hqk', query_part, key_part, preferred_element_type=j...  23.7 us
    all_to_all x1, waiting for transfers between devices, shards(): lax.all_to_all(all_heads.reshape(rows_here, tok_count, heads_here * 2 * h...  23 us
    ppermute x4, waiting for transfers between devices, ring_gather(): lower.append(lax.ppermute(lower[-1] if lower else value, axis, pairs))  12.4 us
    dot_general x1, matrix products, shards(): jnp.dot(hidden, down_weight[0], preferred_element_type=jnp.float32)  11.9 us
  transfers between devices with their start and end apart: 19, of which 12 were waited for; matrix products, arithmetic and copies ran while one was open for 19% of the time, Pallas kernels for 0%

profile of v1, /device:TPU:0, one launch (start us, length us, event | category | flops | bytes accessed | tf_op | source)
XLA Modules:
  0.0 497.8 jit_solution(1079210512942588770)
XLA Ops:
  15.3 2.9 collective-permute-start.4
  19.7 8.0 %all-to-all-start = ((s32[96,16,1]{0,2,1:T(1,128)}), s32[96,16,1]{0,2,1:T(1,128)S(1)}, u32[]{:S(2)}, u32[]{:S(2)}) async-start(s32[96,16,1]{0,2,1:T(1,128)} %broadcast_in_dim.248), calls=%async_computation | async-start | bytes 16384 | tf_op jit(solution)/shard_map/all_to_all | solution.py:243
  32.6 6.2 %collective-permute-done.1 = bf16[192,512]{1,0:T(8,128)(2,1)S(1)} collective-permute-done((bf16[192,512]{1,0:T(8,128)(2,1)S(1)}, bf16[192,512]{1,0:T(8,128)(2,1)S(1)}, u32[]{:S(2)}, u32[]{:S(2)}) %collective-permute-start.1) | collective-permute-done | bytes 196640 | tf_op jit(solution)/shard_map/ppermute | solution.py:24
  39.0 3.0 collective-permute-start.5
  42.0 3.1 collective-permute-done.2
  45.2 3.1 collective-permute-start.6
  48.3 3.1 collective-permute-done.3
  57.7 3.1 copy.56
  60.8 7.2 %all-to-all-start.1 = ((bf16[192,16,256]{2,0,1:T(8,128)(2,1)}), bf16[192,16,256]{2,0,1:T(8,128)(2,1)S(1)}, u32[]{:S(2)}, u32[]{:S(2)}) async-start(bf16[192,16,256]{2,0,1:T(8,128)(2,1)} %copy.56), calls=%async_computation.1 | async-start | bytes 3145728 | tf_op jit(solution)/shard_map/all_to_all | solution.py:215
  72.1 23.0 %all-to-all-done.1 = bf16[192,16,256]{2,0,1:T(8,128)(2,1)S(1)} async-done(((bf16[192,16,256]{2,0,1:T(8,128)(2,1)}), bf16[192,16,256]{2,0,1:T(8,128)(2,1)S(1)}, u32[]{:S(2)}, u32[]{:S(2)}) %all-to-all-start.1) | async-done | bytes 1572896 | tf_op jit(solution)/shard_map/all_to_all | solution.py:215
  98.7 3.5 fusion.141
  102.2 4.5 all-gather.8.cloned.1.call-done
  106.6 4.9 fusion.84
  113.5 4.5 all-to-all-start.2
  118.1 2.7 copy_bitcast_fusion
  120.7 9.9 %all-to-all-done.2 = bf16[96,16,128]{2,0,1:T(8,128)(2,1)S(1)} async-done(((bf16[96,16,128]{2,0,1:T(8,128)(2,1)}), bf16[96,16,128]{2,0,1:T(8,128)(2,1)S(1)}, u32[]{:S(2)}, u32[]{:S(2)}) %all-to-all-start.2) | async-done | bytes 393248 | tf_op jit(solution)/shard_map/all_to_all | solution.py:242
  131.3 18.7 %while.54 = (s32[]{:T(128)}, f32[1,512]{1,0:T(1,128)S(1)}, f32[1,512]{1,0:T(1,128)S(1)}, f32[1,512,128]{2,1,0:T(8,128)}, s32[3072]{0:T(1024)S(1)}, /*index=5*/s3...) while((s32[]{:T(128)}, f32[1,512]{1,0:T(1,128)S(1)}, ...), condition=%wide.region_14.16_spmd.clone, body=%wide.region_11.15_spmd.clone.sunk | while | flops 139135488 | bytes 6226191 | solution.py:138
  151.1 15.0 %while.55 = (s32[]{:T(128)}, f32[1,512]{1,0:T(1,128)S(1)}, f32[1,512]{1,0:T(1,128)S(1)}, f32[1,512,128]{2,1,0:T(8,128)S(1)}, s32[3072]{0:T(1024)S(1)}, /*index=5...) while((s32[]{:T(128)}, f32[1,512]{1,0:T(1,128)S(1)}, ...), condition=%wide.region_18.20_spmd.clone, body=%wide.region_15.19_spmd.clone.sunk | while | flops 139135488 | bytes 4128983 | solution.py:138
  166.3 14.5 %while.56 = (s32[]{:T(128)}, f32[1,512]{1,0:T(1,128)S(1)}, f32[1,512]{1,0:T(1,128)S(1)}, f32[1,512,128]{2,1,0:T(8,128)S(1)}, s32[3072]{0:T(1024)S(1)}, /*index=5...) while((s32[]{:T(128)}, f32[1,512]{1,0:T(1,128)S(1)}, ...), condition=%wide.region_22.24_spmd.clone, body=%wide.region_19.23_spmd.clone.sunk | while | flops 139135488 | bytes 4128983 | solution.py:138
  181.7 3.6 all-to-all-start.3
  185.5 9.2 %all-to-all-done.3 = bf16[16,96,128]{2,1,0:T(8,128)(2,1)S(1)} async-done(((bf16[16,96,128]{2,1,0:T(8,128)(2,1)}), bf16[16,96,128]{2,1,0:T(8,128)(2,1)S(1)}, u32[]{:S(2)}, u32[]{:S(2)}) %all-to-all-start.3) | async-done | bytes 393248 | tf_op jit(solution)/shard_map/all_to_all | solution.py:248
  194.8 4.8 fusion.74
  202.4 61.8 %all-reduce.4.cloned.1.call-done = bf16[192,2048]{1,0:T(8,128)(2,1)} async-done(((bf16[192,2048]{1,0:T(8,128)(2,1)}), bf16[192,2048]{1,0:T(8,128)(2,1)}) %all-reduce.4.cloned.1.call-update) | async-done | bytes 786448 | tf_op jit(solution)/shard_map/psum | solution.py:264
  274.7 60.7 %all-gather.6.cloned.1.call-done = bf16[1536,2048]{1,0:T(8,128)(2,1)} async-done(((bf16[96,2048]{1,0:T(8,128)(2,1)}), bf16[1536,2048]{1,0:T(8,128)(2,1)}) %all-gather.6.cloned.1.call-update) | async-done | bytes 6291472 | tf_op jit(solution)/shard_map/all_gather | solution.py:272
  335.4 7.0 %fusion.82 = f32[1536,352]{0,1:T(8,128)} fusion(bf16[1536,2048]{1,0:T(8,128)(2,1)} %all-gather.6.cloned.1.call-done, bf16[1,2048,352]{1,2,0:T(8,128)(2,1)} %param.35), kind=kOutput, calls=%fused_computation.123 | convolution fusion | flops 2214592512 | bytes 9895936 | tf_op jit(solution)/shard_map/dot_general | solution.py:273
  342.4 11.9 %convolution_convert_fusion.1 = bf16[1536,2048]{1,0:T(8,128)(2,1)} fusion(bf16[1,352,2048]{2,1,0:T(8,128)(2,1)S(1)} %copy-done.15, bf16[1536,2048]{1,0:T(8,128)(2,1)} %all-gather.6.cloned.1.call-done, f32[1536,352]{0,1:T(8,128)} %fusion.82, bf16[1,2048,352]{1,2,0:T(8,128)(2,1)} %param.36), kind=kOutput, calls=%fused_computation.105 | convolution fusion | flops 4435574784 | bytes 17629184 | tf_op jit(solution)/shard_map/dot_general | solution.py:277
  355.0 5.3 %all-to-all-start.4 = ((s32[16,1,1]{2,1,0:T(1,128)}), s32[16,1,1]{2,1,0:T(1,128)S(1)}, u32[]{:S(2)}, u32[]{:S(2)}) async-start(s32[16,1,1]{2,1,0:T(1,128)} %copy.62), calls=%async_computation.6 | async-start | bytes 16384 | tf_op jit(solution)/shard_map/all_to_all | solution.py:204
  362.4 5.4 %all-to-all-done.4 = s32[16,1,1]{2,1,0:T(1,128)S(1)} async-done(((s32[16,1,1]{2,1,0:T(1,128)}), s32[16,1,1]{2,1,0:T(1,128)S(1)}, u32[]{:S(2)}, u32[]{:S(2)}) %all-to-all-start.4) | async-done | bytes 96 | tf_op jit(solution)/shard_map/all_to_all | solution.py:204
  367.8 3.7 all-to-all-start.5
  371.6 83.7 %reduce-scatter.3.cloned.1.call-done = bf16[96,2048]{1,0:T(8,128)(2,1)} async-done(((bf16[1536,2048]{1,0:T(8,128)(2,1)}), bf16[96,2048]{1,0:T(8,128)(2,1)}) %reduce-scatter.3.cloned.1.call-update) | async-done | bytes 393232 | tf_op jit(solution)/shard_map/reduce_scatter | solution.py:276
  455.3 2.8 convolution_convert_fusion.3
  460.9 28.4 %reduce-scatter.5.cloned.1.call-done = bf16[192,256]{1,0:T(8,128)(2,1)} async-done(((bf16[192,2048]{1,0:T(8,128)(2,1)}), bf16[192,256]{1,0:T(8,128)(2,1)}) %reduce-scatter.5.cloned.1.call-update) | async-done | bytes 98320 | tf_op jit(solution)/shard_map/reduce_scatter | solution.py:283
  (356 shorter events, 100.9 us)
Async XLA Ops:
  7.2 3.5 copy-start
  7.2 99.5 %all-gather.8.cloned.1.call-start = ((), (), s32[]{:S(2)}) async-start(), calls=%async_computation.12 | async-start | bytes 8912896 | tf_op jit(solution)/shard_map/all_gather | solution.py:233
  13.3 5.0 %copy-start.11 = (s32[192,2]{0,1:T(2,128)S(1)}, s32[192,2]{0,1:T(2,128)}, u32[]{:S(2)}) copy-start(s32[192,2]{0,1:T(2,128)} %param.38) | copy-start | bytes 4612
  14.1 14.5 %copy-start.12 = (s32[192,2]{0,1:T(2,128)S(1)}, s32[192,2]{0,1:T(2,128)}, u32[]{:S(2)}) copy-start(s32[192,2]{0,1:T(2,128)} %param.39) | copy-start | bytes 4612
  14.1 14.5 %copy-start.9 = (bf16[2048,8]{0,1:T(8,128)(2,1)S(1)}, bf16[2048,8]{0,1:T(8,128)(2,1)}, u32[]{:S(2)}) copy-start(bf16[2048,8]{0,1:T(8,128)(2,1)} %param.29) | copy-start | bytes 98308
  15.3 17.2 %collective-permute-start = (bf16[192,512]{1,0:T(8,128)(2,1)S(1)}, bf16[192,512]{1,0:T(8,128)(2,1)S(1)}, u32[]{:S(2)}, u32[]{:S(2)}) collective-permute-start(bf16[192,512]{1,0:T(8,128)(2,1)S(1)} %convert_element_type.136), channel_id=1, source_target_pairs={{0,1},{1,2},{2,3},{3,4},{4,5},{5,6},{6,7},{7,0},{8,9},{9,10},{10,1... | collective-permute-start | bytes 589832 | tf_op jit(solution)/shard_map/ppermute | solution.py:24
  15.3 23.7 %collective-permute-start.4 = (bf16[192,512]{1,0:T(8,128)(2,1)S(1)}, bf16[192,512]{1,0:T(8,128)(2,1)S(1)}, u32[]{:S(2)}, u32[]{:S(2)}) collective-permute-start(bf16[192,512]{1,0:T(8,128)(2,1)S(1)} %convert_element_type.136), channel_id=1, source_target_pairs={{1,0},{2,1},{3,2},{4,3},{5,4},{6,5},{7,6},{0,7},{9,8},{10,9},{11,1... | collective-permute-start | bytes 589832 | tf_op jit(solution)/shard_map/ppermute | solution.py:26
  19.7 41.1 %all-to-all-start = ((s32[96,16,1]{0,2,1:T(1,128)}), s32[96,16,1]{0,2,1:T(1,128)S(1)}, u32[]{:S(2)}, u32[]{:S(2)}) async-start(s32[96,16,1]{0,2,1:T(1,128)} %broadcast_in_dim.248), calls=%async_computation | async-start | bytes 16384 | tf_op jit(solution)/shard_map/all_to_all | solution.py:243
  27.7 167.1 %all-gather.10.cloned.1.call-start = ((), (), s32[]{:S(2)}) async-start(), calls=%async_computation.13 | async-start | bytes 8912896 | tf_op jit(solution)/shard_map/all_gather | solution.py:258
  32.5 6.3 %collective-permute-start.1 = (bf16[192,512]{1,0:T(8,128)(2,1)S(1)}, bf16[192,512]{1,0:T(8,128)(2,1)S(1)}, u32[]{:S(2)}, u32[]{:S(2)}) collective-permute-start(bf16[192,512]{1,0:T(8,128)(2,1)S(1)} %collective-permute-done), channel_id=1, source_target_pairs={{0,1},{1,2},{2,3},{3,4},{4,5},{5,6},{6,7},{7,0},{8,9},{9,10},{10,1... | collective-permute-start | bytes 589832 | tf_op jit(solution)/shard_map/ppermute | solution.py:24
  38.8 6.3 %collective-permute-start.2 = (bf16[192,512]{1,0:T(8,128)(2,1)S(1)}, bf16[192,512]{1,0:T(8,128)(2,1)S(1)}, u32[]{:S(2)}, u32[]{:S(2)}) collective-permute-start(bf16[192,512]{1,0:T(8,128)(2,1)S(1)} %collective-permute-done.1), channel_id=1, source_target_pairs={{0,1},{1,2},{2,3},{3,4},{4,5},{5,6},{6,7},{7,0},{8,9},{9,10},{10,1... | collective-permute-start | bytes 589832 | tf_op jit(solution)/shard_map/ppermute | solution.py:24
  39.0 6.2 %collective-permute-start.5 = (bf16[192,512]{1,0:T(8,128)(2,1)S(1)}, bf16[192,512]{1,0:T(8,128)(2,1)S(1)}, u32[]{:S(2)}, u32[]{:S(2)}) collective-permute-start(bf16[192,512]{1,0:T(8,128)(2,1)S(1)} %collective-permute-done.4), channel_id=1, source_target_pairs={{1,0},{2,1},{3,2},{4,3},{5,4},{6,5},{7,6},{0,7},{9,8},{10,9},{11,1... | collective-permute-start | bytes 589832 | tf_op jit(solution)/shard_map/ppermute | solution.py:26
  45.1 6.3 %collective-permute-start.3 = (bf16[192,512]{1,0:T(8,128)(2,1)S(1)}, bf16[192,512]{1,0:T(8,128)(2,1)S(1)}, u32[]{:S(2)}, u32[]{:S(2)}) collective-permute-start(bf16[192,512]{1,0:T(8,128)(2,1)S(1)} %collective-permute-done.2), channel_id=1, source_target_pairs={{0,1},{1,2},{2,3},{3,4},{4,5},{5,6},{6,7},{7,0},{8,9},{9,10},{10,1... | collective-permute-start | bytes 589832 | tf_op jit(solution)/shard_map/ppermute | solution.py:24
  45.2 6.4 %collective-permute-start.6 = (bf16[192,512]{1,0:T(8,128)(2,1)S(1)}, bf16[192,512]{1,0:T(8,128)(2,1)S(1)}, u32[]{:S(2)}, u32[]{:S(2)}) collective-permute-start(bf16[192,512]{1,0:T(8,128)(2,1)S(1)} %collective-permute-done.5), channel_id=1, source_target_pairs={{1,0},{2,1},{3,2},{4,3},{5,4},{6,5},{7,6},{0,7},{9,8},{10,9},{11,1... | collective-permute-start | bytes 589832 | tf_op jit(solution)/shard_map/ppermute | solution.py:26
  60.8 34.4 %all-to-all-start.1 = ((bf16[192,16,256]{2,0,1:T(8,128)(2,1)}), bf16[192,16,256]{2,0,1:T(8,128)(2,1)S(1)}, u32[]{:S(2)}, u32[]{:S(2)}) async-start(bf16[192,16,256]{2,0,1:T(8,128)(2,1)} %copy.56), calls=%async_computation.1 | async-start | bytes 3145728 | tf_op jit(solution)/shard_map/all_to_all | solution.py:215
  112.5 5.5 %copy-start.4 = (bf16[3072,1,1,128]{3,2,0,1:T(2,128)(2,1)S(1)}, bf16[3072,1,1,128]{3,2,0,1:T(2,128)(2,1)}, u32[]{:S(2)}) copy-start(bf16[3072,1,1,128]{3,2,0,1:T(2,128)(2,1)} %get-tuple-element.762) | copy-start | bytes 2359300
  113.5 17.1 %all-to-all-start.2 = ((bf16[96,16,128]{2,0,1:T(8,128)(2,1)}), bf16[96,16,128]{2,0,1:T(8,128)(2,1)S(1)}, u32[]{:S(2)}, u32[]{:S(2)}) async-start(bf16[96,16,128]{2,0,1:T(8,128)(2,1)} %pad_maximum_fusion), calls=%async_computation.2 | async-start | bytes 786432 | tf_op jit(solution)/shard_map/all_to_all | solution.py:242
  131.3 19.8 %copy-start.6 = (f32[1,512,128]{2,1,0:T(8,128)S(1)}, f32[1,512,128]{2,1,0:T(8,128)}, u32[]{:S(2)}) copy-start(f32[1,512,128]{2,1,0:T(8,128)} %custom-call.13) | copy-start | bytes 786436
  134.5 1.8 copy-start.7
  137.6 1.8 copy-start.7
  181.7 12.9 %all-to-all-start.3 = ((bf16[16,96,128]{2,1,0:T(8,128)(2,1)}), bf16[16,96,128]{2,1,0:T(8,128)(2,1)S(1)}, u32[]{:S(2)}, u32[]{:S(2)}) async-start(bf16[16,96,128]{2,1,0:T(8,128)(2,1)} %bitcast.30), calls=%async_computation.3 | async-start | bytes 786432 | tf_op jit(solution)/shard_map/all_to_all | solution.py:248
  185.3 78.8 %all-reduce.4.cloned.1.call-start = ((), (), s32[]{:S(2)}) async-start(), calls=%async_computation.8 | async-start | bytes 1572864 | tf_op jit(solution)/shard_map/psum | solution.py:264
  199.7 64.5 %copy-start.2 = (bf16[192,2048]{1,0:T(8,128)(2,1)S(1)}, bf16[192,2048]{1,0:T(8,128)(2,1)}, u32[]{:S(2)}) copy-start(bf16[192,2048]{1,0:T(8,128)(2,1)} %param.27) | copy-start | bytes 2359300
  201.4 134.0 %all-gather.6.cloned.1.call-start = ((), (), s32[]{:S(2)}) async-start(), calls=%async_computation.9 | async-start | bytes 6684672 | tf_op jit(solution)/shard_map/all_gather | solution.py:272
  202.3 64.4 %copy-start.13 = (f32[2048]{0:T(1024)S(1)}, f32[2048]{0:T(1024)}, u32[]{:S(2)}) copy-start(f32[2048]{0:T(1024)} %param.33) | copy-start | bytes 24580
  264.2 2.6 copy-start.5
  274.6 67.8 %copy-start.15 = (bf16[1,352,2048]{2,1,0:T(8,128)(2,1)S(1)}, bf16[1,352,2048]{2,1,0:T(8,128)(2,1)}, u32[]{:S(2)}) copy-start(bf16[1,352,2048]{2,1,0:T(8,128)(2,1)} %param.37) | copy-start | bytes 4325380
  274.6 180.7 %reduce-scatter.3.cloned.1.call-start = ((), (), s32[]{:S(2)}) async-start(), calls=%async_computation.10 | async-start | bytes 6684672 | tf_op jit(solution)/shard_map/reduce_scatter | solution.py:276
  355.0 12.8 %all-to-all-start.4 = ((s32[16,1,1]{2,1,0:T(1,128)}), s32[16,1,1]{2,1,0:T(1,128)S(1)}, u32[]{:S(2)}, u32[]{:S(2)}) async-start(s32[16,1,1]{2,1,0:T(1,128)} %copy.62), calls=%async_computation.6 | async-start | bytes 16384 | tf_op jit(solution)/shard_map/all_to_all | solution.py:204
  367.8 90.7 %all-to-all-start.5 = ((bf16[16,128,512]{2,1,0:T(8,128)(2,1)}), bf16[16,128,512]{2,1,0:T(8,128)(2,1)S(1)}, u32[]{:S(2)}, u32[]{:S(2)}) async-start(bf16[16,128,512]{2,1,0:T(8,128)(2,1)} %bitcast.61), calls=%async_computation.7 | async-start | bytes 4194304 | tf_op jit(solution)/shard_map/all_to_all | solution.py:203
  371.6 117.7 %reduce-scatter.5.cloned.1.call-start = ((), (), s32[]{:S(2)}) async-start(), calls=%async_computation.11 | async-start | bytes 884736 | tf_op jit(solution)/shard_map/reduce_scatter | solution.py:283
  459.7 31.3 %copy-start.1 = (bf16[2048,512]{1,0:T(8,128)(2,1)S(1)}, bf16[2048,512]{1,0:T(8,128)(2,1)}, u32[]{:S(2)}) copy-start(bf16[2048,512]{1,0:T(8,128)(2,1)} %param.30) | copy-start | bytes 6291460
  (14 other events, 15.0 us)
Sparse Core Ops, SparseCore 0:
  10.1 96.5 all-gather.7
  108.8 74.2 all-gather.9
  201.5 62.5 all-reduce.3
  274.7 60.6 all-gather.5
  354.4 100.8 reduce-scatter.2
  458.2 31.0 reduce-scatter.4
